TPU v7x, 32 devices: a whole 2x2x4 slice. The times are simulated.
32 devices in a mesh: dp: 4 (over z), latent: 8 (over y, x, core).
Axes of the slice: x: 2, y: 2, z: 4, core: 2. Of those that a mesh axis runs over, the one named last changes fastest.
Arguments:
- inputs: bfloat16 [64, 2048], P(('dp', 'latent')), may hold values from -6 to 6
- blocks: int32 [64, 4], P(('dp', 'latent')), may hold values from 0 to 127, all different within a row; in each aligned block of 16 rows (0 to 15, 16 to 31, ...) at most 2 rows name the same one
- weights: bfloat16 [8192, 2048], P('latent'), as said below
- enc_bias: float32 [8192], P('latent'), may hold values from -3 to 3
- dec_bias: float32 [2048], replicated, may hold values from -3 to 3
Outputs:
- recon: bfloat16 [64, 2048], P(('dp', 'latent'))
- grad_weights: float32 [8192, 2048], P('latent', 'dp')
- block_scores: float32 [128, 64], P('latent', 'dp')
Inputs may be any that keep to these rules, and one draw needn't show every extreme that they name: Each row names 4 different blocks. Within the rows of one data group (aligned runs of 16 rows) no block is named by more than 2 rows, and some block is named by exactly 2 rows. `weights`: rows have different lengths.
All inputs are finite; a program needn't handle non-finite values.
Results may differ from a plain program's by a relative error of at most 0.0068.
Values may be sent and summed in bfloat16 or wider, within the bound.
No kernel may reach another device: no remote copies, remote signals or barrier semaphores. Data moves between devices by JAX's collectives and lax.ppermute only.
A program may use at most 64 MiB of HBM per device.

v0:
```python
import jax
import jax.numpy as jnp
from jax import lax
from jax.sharding import PartitionSpec as P

BLK = 64
CAP = 2


def local(inputs, blocks, weights, enc_bias, dec_bias):
    lat_rows, width = weights.shape
    block_count = lat_rows // BLK
    centered = (inputs.astype(jnp.float32) - dec_bias).astype(jnp.bfloat16)
    panels, row_lists = (
        lax.all_gather(centered, "latent", axis=0, tiled=True),
        lax.all_gather(blocks, "latent", axis=0, tiled=True),
    )
    rows_group = panels.shape[0]
    squares = jnp.sum(jnp.square(weights.astype(jnp.float32)), axis=1)
    row_norms = jnp.sqrt(squares + 1e-06)
    unit_rows = (weights.astype(jnp.float32) / row_norms[:, None]).astype(jnp.bfloat16)
    unit_blocks = unit_rows.reshape(block_count, BLK, width)
    first_block = lax.axis_index("latent") * block_count
    block_ids = first_block + jnp.arange(block_count, dtype=jnp.int32)
    hit_rows = jnp.any(row_lists[None, :, :] == block_ids[:, None, None], axis=2).astype(jnp.int32)
    before = jnp.cumsum(hit_rows, axis=1) - hit_rows
    slot_ids = jnp.arange(CAP, dtype=jnp.int32)
    picked = (hit_rows[:, None, :] == 1) & (before[:, None, :] == slot_ids[None, :, None])
    row_ids = jnp.sum(
        jnp.where(picked, jnp.arange(rows_group, dtype=jnp.int32)[None, None, :], 0), axis=2
    )
    live_slots = jnp.any(picked, axis=2).astype(jnp.float32)[:, :, None]
    full_dot = jnp.dot(unit_rows, panels.T, preferred_element_type=jnp.float32)
    block_scores = jnp.mean(
        jax.nn.softplus(full_dot + enc_bias[:, None]).reshape(block_count, BLK, rows_group), axis=1
    )
    dot_blocks = full_dot.reshape(block_count, BLK, rows_group)
    base_pre = jnp.transpose(
        jnp.take_along_axis(
            dot_blocks, jnp.broadcast_to(row_ids[:, None, :], (block_count, BLK, CAP)), axis=2
        ),
        (0, 2, 1),
    )
    preact = base_pre + enc_bias.reshape(block_count, BLK)[:, None, :]
    latent_codes = (jax.nn.softplus(preact) * live_slots).astype(jnp.bfloat16)
    slot_rows = panels[row_ids]
    contrib = jnp.einsum(
        "jcm,jmd->jcd", latent_codes, unit_blocks, preferred_element_type=jnp.float32
    )
    partial_value = (
        jnp.zeros((rows_group, width), jnp.float32)
        .at[row_ids.reshape(-1)]
        .add(contrib.reshape(-1, width))
    )
    own_sums = lax.psum_scatter(partial_value, "latent", scatter_dimension=0, tiled=True)
    recon_full = dec_bias + own_sums
    recon_rows = recon_full.astype(jnp.bfloat16)
    errors = (recon_full - inputs.astype(jnp.float32)).astype(jnp.bfloat16)
    all_errors = lax.all_gather(errors, "latent", axis=0, tiled=True)
    slot_errors = all_errors[row_ids]
    code_grad = jnp.einsum(
        "jcd,jmd->jcm", slot_errors, unit_blocks, preferred_element_type=jnp.float32
    )
    pre_grad = (code_grad * jax.nn.sigmoid(preact) * live_slots).astype(jnp.bfloat16)
    along_unit = jnp.sum(
        latent_codes.astype(jnp.float32) * code_grad + pre_grad.astype(jnp.float32) * base_pre,
        axis=1,
    )
    norm_blocks = row_norms.reshape(block_count, BLK)
    groups = lax.axis_size("dp")
    col_count = width // groups
    moved_rows, moved_errors = (
        lax.all_to_all(slot_rows[None], "dp", split_axis=3, concat_axis=0, tiled=True),
        lax.all_to_all(slot_errors[None], "dp", split_axis=3, concat_axis=0, tiled=True),
    )
    got_codes, got_grad = (
        lax.all_gather(latent_codes[None], "dp", axis=0, tiled=True),
        lax.all_gather(pre_grad[None], "dp", axis=0, tiled=True),
    )
    got_along = lax.all_gather(along_unit[None], "dp", axis=0, tiled=True)
    col_start = lax.axis_index("dp") * col_count
    unit_cols = (
        lax.dynamic_slice_in_dim(unit_rows, col_start, col_count, 1)
        .astype(jnp.float32)
        .reshape(block_count, BLK, col_count)
    )
    got_left = jnp.concatenate([got_codes, got_grad], axis=2)
    got_right = jnp.concatenate([moved_errors, moved_rows], axis=2)
    outer_terms = jnp.einsum(
        "gjcm,gjcd->gjmd", got_left, got_right, preferred_element_type=jnp.float32
    )
    group_parts = (outer_terms - unit_cols[None] * got_along[..., None]) / norm_blocks[
        None, :, :, None
    ]
    group_parts = lax.optimization_barrier(group_parts.astype(jnp.bfloat16)).astype(jnp.float32)
    grad_weights = jnp.sum(group_parts, axis=0).reshape(lat_rows, col_count)
    return (recon_rows, grad_weights, block_scores)


def solution(mesh):
    in_specs = (
        P(("dp", "latent"), None),
        P(("dp", "latent"), None),
        P("latent", None),
        P("latent"),
        P(),
    )
    out_specs = (P(("dp", "latent"), None), P("latent", "dp"), P("latent", "dp"))
    return jax.shard_map(local, mesh=mesh, in_specs=in_specs, out_specs=out_specs, check_vma=False)
```

profile of v0, /device:TPU:0, one launch (start us, length us, event | category | flops | bytes accessed | tf_op | source)
XLA Modules:
  0.0 189.1 jit_solution(11037067307001685502)
XLA Ops:
  7.2 10.5 %all-gather.3 = s32[8,2,4]{2,1,0:T(2,128)S(1)} all-gather(s32[1,2,4]{2,1,0:T(2,128)} %bitcast.63), channel_id=1, replica_groups=mesh['dp'=4,'latent'=8] {'latent'}, dimensions={0}, use_global_device_ids=true | all-gather | bytes 288 | tf_op jit(solution)/shard_map/all_gather | solution.py:16
  18.3 0.7 fusion.17
  19.1 9.1 %all-gather.4 = bf16[8,2,2048]{2,1,0:T(2,128)(2,1)S(1)} all-gather(bf16[1,2,2048]{2,1,0:T(2,128)(2,1)S(1)} %fusion.17), channel_id=1, replica_groups=mesh['dp'=4,'latent'=8] {'latent'}, dimensions={0}, use_global_device_ids=true | all-gather | bytes 73728 | tf_op jit(solution)/shard_map/all_gather | solution.py:15
  29.0 0.8 copy.75
  29.7 1.7 reshape.170
  31.5 4.9 %all-to-all-start.1 = ((bf16[4,2,8192]{2,1,0:T(2,128)(2,1)}), bf16[4,2,8192]{2,1,0:T(2,128)(2,1)}, u32[]{:S(2)}, u32[]{:S(2)}) async-start(bf16[4,2,8192]{2,1,0:T(2,128)(2,1)} %reshape.170), calls=%async_computation.1 | async-start | bytes 262144 | tf_op jit(solution)/shard_map/all_to_all | solution.py:73
  36.6 0.7 copy.65
  38.0 3.1 %fusion = f32[1024]{0:T(1024)S(1)} fusion(bf16[1024,2048]{1,0:T(8,128)(2,1)} %param.7), kind=kLoop, calls=%fused_computation.6 | loop fusion | flops 6290432 | bytes 4198400 | tf_op jit(solution)/shard_map/reduce_sum | solution.py:19
  41.8 0.7 copy.70
  43.6 3.9 %fusion.1 = bf16[1024,2048]{1,0:T(8,128)(2,1)S(1)} fusion(bf16[1024,2048]{1,0:T(8,128)(2,1)} %param.7, f32[1024]{0:T(1024)S(1)} %add_sqrt_fusion), kind=kLoop, calls=%fused_computation.7 | loop fusion | flops 6291456 | bytes 8392704 | tf_op jit(solution)/shard_map/convert_element_type | solution.py:21
  47.5 2.0 %compare_select_fusion = (f32[1024,16]{0,1:T(8,128)}, f32[1024,16]{0,1:T(8,128)S(1)}) fusion(f32[1024]{0:T(1024)S(1)} %copy-done.2, bf16[1024,2048]{1,0:T(8,128)(2,1)S(1)} %fusion.1, bf16[16,2048]{1,0:T(8,128)(2,1)S(1)} %reshape.164), kind=kOutput, calls=%fused_computation.13 | convolution fusion | flops 67223552 | bytes 4395008 | tf_op jit(solution)/shard_map/dot_general | solution.py:33
  49.6 16.8 %gather_fusion.2 = f32[2048]{0:T(1024)S(1)} fusion(f32[16,64,16]{1,0,2:T(8,128)S(1)} %reshape.118, s32[2048]{0:T(1024)S(1)} %reshape.140), kind=kCustom, calls=%fused_computation.2 | custom fusion | bytes 40960 | tf_op jit(solution)/shard_map/jit(take_along_axis)/gather | solution.py:39
  67.4 2.8 %fusion.21 = f32[16,2,2048]{2,1,0:T(2,128)S(1)} fusion(bf16[16,2,64]{2,1,0:T(2,128)(2,1)S(1)} %get-tuple-element.14, bf16[16,64,2048]{2,1,0:T(8,128)(2,1)} %bitcast.49), kind=kOutput, calls=%fused_computation.53 | convolution fusion | flops 8388608 | bytes 4460544 | tf_op jit(solution)/shard_map/jcm,jmd->jcd/dot_general | solution.py:47
  70.4 1.7 scatter_custom_fusion
  72.4 1.3 constant_dynamic-slice_fusion
  73.8 0.7 copy.78
  76.0 13.7 %all-gather = bf16[64,2,64]{2,1,0:T(2,128)(2,1)S(1)} all-gather(bf16[16,2,64]{2,1,0:T(2,128)(2,1)S(1)} %get-tuple-element.14), channel_id=2, replica_groups=mesh['dp'=4,'latent'=8] {'dp'}, dimensions={0}, use_global_device_ids=true | all-gather | bytes 20480 | tf_op jit(solution)/shard_map/all_gather | solution.py:77
  89.7 36.1 %all-reduce.3.cloned.1.call-done = f32[16,2048]{1,0:T(8,128)} async-done(((f32[16,2048]{1,0:T(8,128)}), f32[16,2048]{1,0:T(8,128)}) %all-reduce.3.cloned.1.call-update) | async-done | bytes 131088
  125.7 1.5 fusion.18
  127.2 8.7 %all-gather.5 = bf16[8,2,2048]{2,1,0:T(2,128)(2,1)S(1)} all-gather(bf16[1,2,2048]{2,1,0:T(2,128)(2,1)S(1)} %get-tuple-element.16), channel_id=1, replica_groups=mesh['dp'=4,'latent'=8] {'latent'}, dimensions={0}, use_global_device_ids=true | all-gather | bytes 73728 | tf_op jit(solution)/shard_map/all_gather | solution.py:59
  136.8 0.8 copy.72
  137.6 1.7 reshape.172
  139.3 4.6 %all-to-all-start = ((bf16[4,2,8192]{2,1,0:T(2,128)(2,1)}), bf16[4,2,8192]{2,1,0:T(2,128)(2,1)S(1)}, u32[]{:S(2)}, u32[]{:S(2)}) async-start(bf16[4,2,8192]{2,1,0:T(2,128)(2,1)} %reshape.172), calls=%async_computation | async-start | bytes 262144 | tf_op jit(solution)/shard_map/all_to_all | solution.py:74
  143.9 3.4 %add_reduce_fusion = (f32[16,64]{1,0:T(8,128)S(1)}, bf16[16,2,64]{2,1,0:T(2,128)(2,1)S(1)}) fusion(f32[16,2,64]{2,1,0:T(2,128)S(1)} %get-tuple-element.15, bf16[16,2,64]{2,1,0:T(2,128)(2,1)S(1)} %get-tuple-element.14, f32[16,2]{1,0:T(8,128)S(1)} %copy-done.12, f32[16,64]{1,0:T(8,128)S(1)} %copy-done.11, bf16[16,2,2048]{2,1,0:T(2,128)(2,1)S(1)} %reshape.125, ...), kind=kOutput, calls=%fused_computation.31 | convolution fusion | flops 8414208 | bytes 4350080 | tf_op jit(solution)/shard_map/jcd,jmd->jcm/dot_general | solution.py:61
  147.3 13.7 %all-gather.2 = f32[64,64]{1,0:T(8,128)S(1)} all-gather(f32[16,64]{1,0:T(8,128)S(1)} %get-tuple-element.12), channel_id=4, replica_groups=mesh['dp'=4,'latent'=8] {'dp'}, dimensions={0}, use_global_device_ids=true | all-gather | bytes 20480 | tf_op jit(solution)/shard_map/all_gather | solution.py:80
  161.0 13.1 %all-gather.1 = bf16[64,2,64]{2,1,0:T(2,128)(2,1)S(1)} all-gather(bf16[16,2,64]{2,1,0:T(2,128)(2,1)S(1)} %get-tuple-element.13), channel_id=3, replica_groups=mesh['dp'=4,'latent'=8] {'dp'}, dimensions={0}, use_global_device_ids=true | all-gather | bytes 20480 | tf_op jit(solution)/shard_map/all_gather | solution.py:78
  174.1 1.6 reshape.171
  175.8 0.7 copy.77
  176.5 0.7 reshape.173
  177.2 0.7 copy.74
  178.0 2.1 %divide_convert_fusion = bf16[4,16,64,512]{3,2,1,0:T(8,128)(2,1)S(1)} fusion(f32[16,64]{1,0:T(8,128)S(1)} %sqrt.15, f32[4,16,64]{2,1,0:T(8,128)S(1)} %bitcast.60, f32[16,64,512]{2,1,0:T(8,128)S(1)} %convert.1, bf16[4,16,2,512]{3,2,1,0:T(2,128)(2,1)S(1)} %bitcast.57, bf16[4,16,2,512]{3,2,1,0:T(2,128)(2,1)S(1)} %bitcast.58, ...), kind=kOutput, calls=%fused_computation.9 | convolution fusion | flops 25755648 | bytes 6606848 | tf_op jit(solution)/shard_map/gjcm,gjcd->gjmd/dot_general | solution.py:89
  180.1 2.1 %convert_reduce_fusion = f32[16,64,512]{2,1,0:T(8,128)} fusion(bf16[4,16,64,512]{3,2,1,0:T(8,128)(2,1)S(1)} %divide_convert_fusion), kind=kLoop, calls=%fused_computation.8 | loop fusion | flops 3670016 | bytes 6291456 | tf_op jit(solution)/shard_map/reduce_sum | solution.py:96
  (78 shorter events, 7.4 us)
Async XLA Ops:
  18.3 10.5 %copy-start.3 = (s32[1024]{0:T(1024)}, s32[1024]{0:T(1024)S(1)}, u32[]{:S(2)}) copy-start(s32[1024]{0:T(1024)S(1)} %pad_clamp_fusion) | copy-start | bytes 12292
  28.2 12.9 %copy-start.2 = (f32[1024]{0:T(1024)S(1)}, f32[1024]{0:T(1024)}, u32[]{:S(2)}) copy-start(f32[1024]{0:T(1024)} %param.8) | copy-start | bytes 12292
  31.5 107.9 %all-to-all-start.1 = ((bf16[4,2,8192]{2,1,0:T(2,128)(2,1)}), bf16[4,2,8192]{2,1,0:T(2,128)(2,1)}, u32[]{:S(2)}, u32[]{:S(2)}) async-start(bf16[4,2,8192]{2,1,0:T(2,128)(2,1)} %reshape.170), calls=%async_computation.1 | async-start | bytes 262144 | tf_op jit(solution)/shard_map/all_to_all | solution.py:73
  36.3 89.4 %all-reduce.3.cloned.1.call-start = ((), (), s32[]{:S(2)}) async-start(), calls=%async_computation.2 | async-start | bytes 262144
  36.6 6.5 %copy-start.5 = (s32[16,2]{1,0:T(8,128)}, s32[16,2]{1,0:T(8,128)S(1)}, u32[]{:S(2)}) copy-start(s32[16,2]{1,0:T(8,128)S(1)} %copy.64) | copy-start | bytes 388
  41.1 6.4 %copy-start.7 = (f32[1024]{0:T(1024)}, f32[1024]{0:T(1024)S(1)}, u32[]{:S(2)}) copy-start(f32[1024]{0:T(1024)S(1)} %add_sqrt_fusion) | copy-start | bytes 12292
  47.5 2.0 %copy-start = (bf16[1024,2048]{1,0:T(8,128)(2,1)}, bf16[1024,2048]{1,0:T(8,128)(2,1)S(1)}, u32[]{:S(2)}) copy-start(bf16[1024,2048]{1,0:T(8,128)(2,1)S(1)} %fusion.1) | copy-start | bytes 12582916
  49.6 17.6 %copy-start.6 = (s32[16,2]{1,0:T(8,128)S(1)}, s32[16,2]{1,0:T(8,128)}, u32[]{:S(2)}) copy-start(s32[16,2]{1,0:T(8,128)} %copy-done.5) | copy-start | bytes 388
  49.6 17.6 %copy-start.11 = (f32[16,64]{1,0:T(8,128)S(1)}, f32[16,64]{1,0:T(8,128)}, u32[]{:S(2)}) copy-start(f32[16,64]{1,0:T(8,128)} %add.114) | copy-start | bytes 12292
  49.6 17.6 %copy-start.12 = (f32[16,2]{1,0:T(8,128)S(1)}, f32[16,2]{1,0:T(8,128)}, u32[]{:S(2)}) copy-start(f32[16,2]{1,0:T(8,128)} %copy.70) | copy-start | bytes 388
  49.6 17.6 %copy-start.13 = (s32[16,2]{1,0:T(8,128)S(1)}, s32[16,2]{1,0:T(8,128)}, u32[]{:S(2)}) copy-start(s32[16,2]{1,0:T(8,128)} %copy.66) | copy-start | bytes 388
  49.6 17.6 %copy-start.14 = (pred[16,2]{1,0:T(8,128)(4,1)S(1)}, pred[16,2]{1,0:T(8,128)(4,1)}, u32[]{:S(2)}) copy-start(pred[16,2]{1,0:T(8,128)(4,1)} %copy.65) | copy-start | bytes 100
  66.5 5.7 %copy-start.1 = (f32[1024,16]{0,1:T(8,128)S(1)}, f32[1024,16]{0,1:T(8,128)}, u32[]{:S(2)}) copy-start(f32[1024,16]{0,1:T(8,128)} %get-tuple-element.20) | copy-start | bytes 196612
  66.9 6.8 %copy-start.8 = (f32[1024]{0:T(1024)S(1)}, f32[1024]{0:T(1024)}, u32[]{:S(2)}) copy-start(f32[1024]{0:T(1024)} %copy-done.7) | copy-start | bytes 12292
  70.2 4.5 %copy-start.15 = (u32[32]{0:T(128)S(1)}, u32[32]{0:T(128)}, u32[]{:S(2)}) copy-start(u32[32]{0:T(128)} %constant.78) | copy-start | bytes 388
  70.2 55.5 %copy-start.9 = (bf16[2,2048]{1,0:T(2,128)(2,1)S(1)}, bf16[2,2048]{1,0:T(2,128)(2,1)}, u32[]{:S(2)}) copy-start(bf16[2,2048]{1,0:T(2,128)(2,1)} %param.5) | copy-start | bytes 24580
  70.2 55.5 %copy-start.10 = (f32[2048]{0:T(1024)S(1)}, f32[2048]{0:T(1024)}, u32[]{:S(2)}) copy-start(f32[2048]{0:T(1024)} %param.9) | copy-start | bytes 24580
  70.2 65.7 %copy-start.4 = (s32[1024]{0:T(1024)S(1)}, s32[1024]{0:T(1024)}, u32[]{:S(2)}) copy-start(s32[1024]{0:T(1024)} %copy-done.3) | copy-start | bytes 12292
  139.3 37.2 %all-to-all-start = ((bf16[4,2,8192]{2,1,0:T(2,128)(2,1)}), bf16[4,2,8192]{2,1,0:T(2,128)(2,1)S(1)}, u32[]{:S(2)}, u32[]{:S(2)}) async-start(bf16[4,2,8192]{2,1,0:T(2,128)(2,1)} %reshape.172), calls=%async_computation | async-start | bytes 262144 | tf_op jit(solution)/shard_map/all_to_all | solution.py:74
Sparse Core Ops, SparseCore 0:
  72.3 53.3 all-reduce.2
where the time goes:
time: 190 us; the launch traced here: 189 us
  blocking collectives  68.8 us (36%)
  waiting for transfers between devices  36.1 us (19%)
  local copies, waits for them, and re-layouts  34.6 us (18%)
  between operations  15.1 us (8%)
  other arithmetic  14.7 us (8%)
  matrix products  10.3 us (5%)
  starting transfers between devices  9.47 us (5%)
    unnamed x2, waiting for transfers between devices  36.1 us
    gather x5, local copies, waits for them, and re-layouts, local(): jnp.take_along_axis(dot_blocks, jnp.broadcast_to(row_ids[:, None, :], (bl...  18 us
    all_gather x1, blocking collectives, local(): got_along = lax.all_gather(along_unit[None], 'dp', axis=0, tiled=True)  13.7 us
    all_gather x1, blocking collectives, local(): lax.all_gather(latent_codes[None], 'dp', axis=0, tiled=True)  13.7 us
    all_gather x1, blocking collectives, local(): lax.all_gather(pre_grad[None], 'dp', axis=0, tiled=True)  13.1 us
    all_gather x1, blocking collectives, local(): lax.all_gather(blocks, 'latent', axis=0, tiled=True)  10.5 us
    all_gather x1, blocking collectives, local(): lax.all_gather(centered, 'latent', axis=0, tiled=True)  9.08 us
    all_gather x1, blocking collectives, local(): all_errors = lax.all_gather(errors, 'latent', axis=0, tiled=True)  8.72 us
  transfers between devices with their start and end apart: 3, of which 1 were waited for; matrix products, arithmetic and copies ran while one was open for 26% of the time, Pallas kernels for 0%

commit v1 on v0

--- a/solution.py
+++ b/solution.py
@@ -5,6 +5,18 @@
 
 BLK = 64
 CAP = 2
+
+
+def doubled_up(value, axis, dim):
+    ways, here, turn = (lax.axis_size(axis), lax.axis_index(axis), value.shape[dim])
+    line, have = (value, 1)
+    while have < ways:
+        line = jnp.concatenate(
+            [line, lax.ppermute(line, axis, [(d, (d - have) % ways) for d in range(ways)])],
+            axis=dim,
+        )
+        have = 2 * have
+    return jnp.roll(line, here * turn, axis=dim)
 
 
 def local(inputs, blocks, weights, enc_bias, dec_bias):
@@ -75,7 +87,7 @@
     )
     got_codes, got_grad = (
         lax.all_gather(latent_codes[None], "dp", axis=0, tiled=True),
-        lax.all_gather(pre_grad[None], "dp", axis=0, tiled=True),
+        doubled_up(pre_grad[None], "dp", 0),
     )
     got_along = lax.all_gather(along_unit[None], "dp", axis=0, tiled=True)
     col_start = lax.axis_index("dp") * col_count

time: 190 us -> 187 us (0.984)
  blocking collectives: 68.8 us -> 54.9 us
  waiting for transfers between devices: 36.1 us -> 43.6 us
  starting transfers between devices: 9.47 us -> 12.4 us
    all_gather x1 -> x0, blocking collectives: 13.1 us -> none  [local(): lax.all_gather(pre_grad[None], 'dp', axis=0, tiled=True)]
    ppermute x0 -> x2, starting transfers between devices: none -> 4.2 us  [doubled_up(): lax.ppermute(line, axis, [(d, (d - have) % ways) for d in range(ways)])]
    ppermute x0 -> x2, waiting for transfers between devices: none -> 4.05 us  [doubled_up(): lax.ppermute(line, axis, [(d, (d - have) % ways) for d in range(ways)])]
    all_to_all x1, waiting for transfers between devices: 0.01 us -> 3.45 us  [local(): lax.all_to_all(slot_errors[None], 'dp', split_axis=3, concat_axis=0, tile...]
    unnamed x41 -> x45, local copies, waits for them, and re-layouts: 7.23 us -> 7.3 us
  transfers between devices with their start and end apart: 3 -> 5, of which waited for: 1 -> 3; matrix products, arithmetic and copies ran while one was open for 26% -> 27% of each run, Pallas kernels for 0% -> 0%
where the time goes in v1:
time: 187 us; the launch traced here: 186 us
  blocking collectives  54.9 us (29%)
  waiting for transfers between devices  43.6 us (23%)
  local copies, waits for them, and re-layouts  34.7 us (19%)
  between operations  15.2 us (8%)
  other arithmetic  14.7 us (8%)
  starting transfers between devices  12.4 us (7%)
  matrix products  10.3 us (6%)
    unnamed x2, waiting for transfers between devices  36.1 us
    gather x5, local copies, waits for them, and re-layouts, local(): jnp.take_along_axis(dot_blocks, jnp.broadcast_to(row_ids[:, None, :], (bl...  18 us
    all_gather x1, blocking collectives, local(): lax.all_gather(latent_codes[None], 'dp', axis=0, tiled=True)  13.7 us
    all_gather x1, blocking collectives, local(): got_along = lax.all_gather(along_unit[None], 'dp', axis=0, tiled=True)  13.1 us
    all_gather x1, blocking collectives, local(): lax.all_gather(blocks, 'latent', axis=0, tiled=True)  10.5 us
    all_gather x1, blocking collectives, local(): lax.all_gather(centered, 'latent', axis=0, tiled=True)  9.08 us
    all_gather x1, blocking collectives, local(): all_errors = lax.all_gather(errors, 'latent', axis=0, tiled=True)  8.54 us
    unnamed x45, local copies, waits for them, and re-layouts  7.3 us
  transfers between devices with their start and end apart: 5, of which 3 were waited for; matrix products, arithmetic and copies ran while one was open for 27% of the time, Pallas kernels for 0%

profile of v1, /device:TPU:0, one launch (start us, length us, event | category | flops | bytes accessed | tf_op | source)
XLA Modules:
  0.0 185.8 jit_solution(11527382754691550173)
XLA Ops:
  7.2 10.5 %all-gather.2 = s32[8,2,4]{2,1,0:T(2,128)S(1)} all-gather(s32[1,2,4]{2,1,0:T(2,128)} %bitcast.66), channel_id=1, replica_groups=mesh['dp'=4,'latent'=8] {'latent'}, dimensions={0}, use_global_device_ids=true | all-gather | bytes 288 | tf_op jit(solution)/shard_map/all_gather | solution.py:28
  18.3 0.7 fusion.17
  19.1 9.1 %all-gather.3 = bf16[8,2,2048]{2,1,0:T(2,128)(2,1)S(1)} all-gather(bf16[1,2,2048]{2,1,0:T(2,128)(2,1)S(1)} %fusion.17), channel_id=1, replica_groups=mesh['dp'=4,'latent'=8] {'latent'}, dimensions={0}, use_global_device_ids=true | all-gather | bytes 73728 | tf_op jit(solution)/shard_map/all_gather | solution.py:27
  29.0 0.8 copy.75
  29.7 1.7 reshape.169
  31.5 4.9 %all-to-all-start.1 = ((bf16[4,2,8192]{2,1,0:T(2,128)(2,1)}), bf16[4,2,8192]{2,1,0:T(2,128)(2,1)}, u32[]{:S(2)}, u32[]{:S(2)}) async-start(bf16[4,2,8192]{2,1,0:T(2,128)(2,1)} %reshape.169), calls=%async_computation.1 | async-start | bytes 262144 | tf_op jit(solution)/shard_map/all_to_all | solution.py:85
  38.0 3.1 %fusion = f32[1024]{0:T(1024)S(1)} fusion(bf16[1024,2048]{1,0:T(8,128)(2,1)} %param.7), kind=kLoop, calls=%fused_computation.6 | loop fusion | flops 6290432 | bytes 4198400 | tf_op jit(solution)/shard_map/reduce_sum | solution.py:31
  41.8 0.7 copy.70
  43.6 3.9 %fusion.1 = bf16[1024,2048]{1,0:T(8,128)(2,1)S(1)} fusion(bf16[1024,2048]{1,0:T(8,128)(2,1)} %param.7, f32[1024]{0:T(1024)S(1)} %add_sqrt_fusion), kind=kLoop, calls=%fused_computation.7 | loop fusion | flops 6291456 | bytes 8392704 | tf_op jit(solution)/shard_map/convert_element_type | solution.py:33
  47.5 2.0 %compare_select_fusion = (f32[1024,16]{0,1:T(8,128)}, f32[1024,16]{0,1:T(8,128)S(1)}) fusion(f32[1024]{0:T(1024)S(1)} %copy-done.2, bf16[1024,2048]{1,0:T(8,128)(2,1)S(1)} %fusion.1, bf16[16,2048]{1,0:T(8,128)(2,1)S(1)} %reshape.163), kind=kOutput, calls=%fused_computation.13 | convolution fusion | flops 67223552 | bytes 4395008 | tf_op jit(solution)/shard_map/dot_general | solution.py:45
  49.6 16.8 %gather_fusion.2 = f32[2048]{0:T(1024)S(1)} fusion(f32[16,64,16]{1,0,2:T(8,128)S(1)} %reshape.118, s32[2048]{0:T(1024)S(1)} %reshape.140), kind=kCustom, calls=%fused_computation.2 | custom fusion | bytes 40960 | tf_op jit(solution)/shard_map/jit(take_along_axis)/gather | solution.py:51
  67.4 2.8 %fusion.21 = f32[16,2,2048]{2,1,0:T(2,128)S(1)} fusion(bf16[16,2,64]{2,1,0:T(2,128)(2,1)S(1)} %get-tuple-element.14, bf16[16,64,2048]{2,1,0:T(8,128)(2,1)} %bitcast.51), kind=kOutput, calls=%fused_computation.61 | convolution fusion | flops 8388608 | bytes 4460544 | tf_op jit(solution)/shard_map/jcm,jmd->jcd/dot_general | solution.py:59
  70.4 1.7 scatter_custom_fusion
  72.4 1.3 constant_dynamic-slice_fusion
  76.0 13.7 %all-gather = bf16[64,2,64]{2,1,0:T(2,128)(2,1)S(1)} all-gather(bf16[16,2,64]{2,1,0:T(2,128)(2,1)S(1)} %get-tuple-element.14), channel_id=2, replica_groups=mesh['dp'=4,'latent'=8] {'dp'}, dimensions={0}, use_global_device_ids=true | all-gather | bytes 20480 | tf_op jit(solution)/shard_map/all_gather | solution.py:89
  89.7 36.1 %all-reduce.3.cloned.1.call-done = f32[16,2048]{1,0:T(8,128)} async-done(((f32[16,2048]{1,0:T(8,128)}), f32[16,2048]{1,0:T(8,128)}) %all-reduce.3.cloned.1.call-update) | async-done | bytes 131088
  125.7 1.5 fusion.18
  127.2 8.5 %all-gather.4 = bf16[8,2,2048]{2,1,0:T(2,128)(2,1)S(1)} all-gather(bf16[1,2,2048]{2,1,0:T(2,128)(2,1)S(1)} %get-tuple-element.16), channel_id=1, replica_groups=mesh['dp'=4,'latent'=8] {'latent'}, dimensions={0}, use_global_device_ids=true | all-gather | bytes 73728 | tf_op jit(solution)/shard_map/all_gather | solution.py:71
  136.6 3.4 %constant_dynamic-update-slice_fusion.5 = (bf16[8,16,2,64]{3,2,1,0:T(2,128)(2,1)S(1)}, bf16[16,2,64]{2,1,0:T(2,128)(2,1)S(1)}, f32[16,2,64]{2,1,0:T(2,128)S(1)}) fusion(f32[16,2]{1,0:T(8,128)S(1)} %copy-done.12, f32[16,2,64]{2,1,0:T(2,128)S(1)} %get-tuple-element.15, f32[16,64]{1,0:T(8,128)S(1)} %copy-done.11, bf16[16,2,2048]{2,1,0:T(2,128)(2,1)S(1)} %reshape.125, ...), kind=kOutput, calls=%fused_computation.43 | convolution fusion | flops 8402943 | bytes 4370560 | tf_op jit(solution)/shard_map/jcd,jmd->jcm/dot_general | solution.py:73
  140.1 3.6 %collective-permute-start = (bf16[1,16,2,64]{3,2,1,0:T(2,128)(2,1)S(1)}, bf16[1,16,2,64]{3,2,1,0:T(2,128)(2,1)S(1)}, u32[]{:S(2)}, u32[]{:S(2)}) collective-permute-start(bf16[1,16,2,64]{3,2,1,0:T(2,128)(2,1)S(1)} %bitcast.61), channel_id=1, source_target_pairs={{0,24},{8,0},{16,8},{24,16},{1,25},{9,1},{17,9},{25,17},{2,26},{10... | collective-permute-start | bytes 12296 | tf_op jit(solution)/shard_map/ppermute | solution.py:15
  143.6 0.8 copy.72
  144.4 1.7 reshape.171
  146.1 13.1 %all-gather.1 = f32[64,64]{1,0:T(8,128)S(1)} all-gather(f32[16,64]{1,0:T(8,128)S(1)} %add_reduce_fusion), channel_id=3, replica_groups=mesh['dp'=4,'latent'=8] {'dp'}, dimensions={0}, use_global_device_ids=true | all-gather | bytes 20480 | tf_op jit(solution)/shard_map/all_gather | solution.py:92
  159.9 4.0 %collective-permute-done.1 = bf16[2,16,2,64]{3,2,1,0:T(2,128)(2,1)S(1)} collective-permute-done((bf16[2,16,2,64]{3,2,1,0:T(2,128)(2,1)S(1)}, bf16[2,16,2,64]{3,2,1,0:T(2,128)(2,1)S(1)}, u32[]{:S(2)}, u32[]{:S(2)}) %collective-permute-start.1) | collective-permute-done | bytes 8224 | tf_op jit(solution)/shard_map/ppermute | solution.py:15
  164.1 3.3 %all-to-all-start = ((bf16[4,2,8192]{2,1,0:T(2,128)(2,1)}), bf16[4,2,8192]{2,1,0:T(2,128)(2,1)S(1)}, u32[]{:S(2)}, u32[]{:S(2)}) async-start(bf16[4,2,8192]{2,1,0:T(2,128)(2,1)} %reshape.171), calls=%async_computation | async-start | bytes 262144 | tf_op jit(solution)/shard_map/all_to_all | solution.py:86
  167.5 1.6 reshape.170
  169.1 0.7 copy.77
  169.8 3.4 %all-to-all-done = bf16[4,2,8192]{2,1,0:T(2,128)(2,1)S(1)} async-done(((bf16[4,2,8192]{2,1,0:T(2,128)(2,1)}), bf16[4,2,8192]{2,1,0:T(2,128)(2,1)S(1)}, u32[]{:S(2)}, u32[]{:S(2)}) %all-to-all-start) | async-done | bytes 131104 | tf_op jit(solution)/shard_map/all_to_all | solution.py:86
  173.3 0.7 reshape.172
  174.0 0.7 copy.74
  174.7 2.1 %divide_convert_fusion = bf16[4,16,64,512]{3,2,1,0:T(8,128)(2,1)S(1)} fusion(f32[16,64]{1,0:T(8,128)S(1)} %sqrt.15, f32[4,16,64]{2,1,0:T(8,128)S(1)} %bitcast.64, f32[16,64,512]{2,1,0:T(8,128)S(1)} %convert.1, bf16[4,16,2,512]{3,2,1,0:T(2,128)(2,1)S(1)} %bitcast.59, bf16[4,16,2,512]{3,2,1,0:T(2,128)(2,1)S(1)} %bitcast.60, ...), kind=kOutput, calls=%fused_computation.9 | convolution fusion | flops 25755648 | bytes 6606848 | tf_op jit(solution)/shard_map/gjcm,gjcd->gjmd/dot_general | solution.py:101
  176.8 2.1 %convert_reduce_fusion = f32[16,64,512]{2,1,0:T(8,128)} fusion(bf16[4,16,64,512]{3,2,1,0:T(8,128)(2,1)S(1)} %divide_convert_fusion), kind=kLoop, calls=%fused_computation.8 | loop fusion | flops 3670016 | bytes 6291456 | tf_op jit(solution)/shard_map/reduce_sum | solution.py:108
  (89 shorter events, 9.6 us)
Async XLA Ops:
  18.3 10.5 %copy-start.3 = (s32[1024]{0:T(1024)}, s32[1024]{0:T(1024)S(1)}, u32[]{:S(2)}) copy-start(s32[1024]{0:T(1024)S(1)} %pad_clamp_fusion) | copy-start | bytes 12292
  28.2 12.9 %copy-start.2 = (f32[1024]{0:T(1024)S(1)}, f32[1024]{0:T(1024)}, u32[]{:S(2)}) copy-start(f32[1024]{0:T(1024)} %param.8) | copy-start | bytes 12292
  31.5 132.6 %all-to-all-start.1 = ((bf16[4,2,8192]{2,1,0:T(2,128)(2,1)}), bf16[4,2,8192]{2,1,0:T(2,128)(2,1)}, u32[]{:S(2)}, u32[]{:S(2)}) async-start(bf16[4,2,8192]{2,1,0:T(2,128)(2,1)} %reshape.169), calls=%async_computation.1 | async-start | bytes 262144 | tf_op jit(solution)/shard_map/all_to_all | solution.py:85
  36.3 89.4 %all-reduce.3.cloned.1.call-start = ((), (), s32[]{:S(2)}) async-start(), calls=%async_computation.2 | async-start | bytes 262144
  36.6 6.5 %copy-start.5 = (s32[16,2]{1,0:T(8,128)}, s32[16,2]{1,0:T(8,128)S(1)}, u32[]{:S(2)}) copy-start(s32[16,2]{1,0:T(8,128)S(1)} %copy.64) | copy-start | bytes 388
  41.1 6.4 %copy-start.7 = (f32[1024]{0:T(1024)}, f32[1024]{0:T(1024)S(1)}, u32[]{:S(2)}) copy-start(f32[1024]{0:T(1024)S(1)} %add_sqrt_fusion) | copy-start | bytes 12292
  47.5 2.0 %copy-start = (bf16[1024,2048]{1,0:T(8,128)(2,1)}, bf16[1024,2048]{1,0:T(8,128)(2,1)S(1)}, u32[]{:S(2)}) copy-start(bf16[1024,2048]{1,0:T(8,128)(2,1)S(1)} %fusion.1) | copy-start | bytes 12582916
  49.6 17.6 %copy-start.6 = (s32[16,2]{1,0:T(8,128)S(1)}, s32[16,2]{1,0:T(8,128)}, u32[]{:S(2)}) copy-start(s32[16,2]{1,0:T(8,128)} %copy-done.5) | copy-start | bytes 388
  49.6 17.6 %copy-start.11 = (f32[16,64]{1,0:T(8,128)S(1)}, f32[16,64]{1,0:T(8,128)}, u32[]{:S(2)}) copy-start(f32[16,64]{1,0:T(8,128)} %add.124) | copy-start | bytes 12292
  49.6 17.6 %copy-start.12 = (f32[16,2]{1,0:T(8,128)S(1)}, f32[16,2]{1,0:T(8,128)}, u32[]{:S(2)}) copy-start(f32[16,2]{1,0:T(8,128)} %copy.70) | copy-start | bytes 388
  49.6 17.6 %copy-start.13 = (s32[16,2]{1,0:T(8,128)S(1)}, s32[16,2]{1,0:T(8,128)}, u32[]{:S(2)}) copy-start(s32[16,2]{1,0:T(8,128)} %copy.66) | copy-start | bytes 388
  49.6 17.6 %copy-start.14 = (pred[16,2]{1,0:T(8,128)(4,1)S(1)}, pred[16,2]{1,0:T(8,128)(4,1)}, u32[]{:S(2)}) copy-start(pred[16,2]{1,0:T(8,128)(4,1)} %copy.65) | copy-start | bytes 100
  66.5 5.7 %copy-start.1 = (f32[1024,16]{0,1:T(8,128)S(1)}, f32[1024,16]{0,1:T(8,128)}, u32[]{:S(2)}) copy-start(f32[1024,16]{0,1:T(8,128)} %get-tuple-element.21) | copy-start | bytes 196612
  66.9 6.8 %copy-start.8 = (f32[1024]{0:T(1024)S(1)}, f32[1024]{0:T(1024)}, u32[]{:S(2)}) copy-start(f32[1024]{0:T(1024)} %copy-done.7) | copy-start | bytes 12292
  70.2 4.5 %copy-start.15 = (u32[32]{0:T(128)S(1)}, u32[32]{0:T(128)}, u32[]{:S(2)}) copy-start(u32[32]{0:T(128)} %constant.99) | copy-start | bytes 388
  70.2 55.5 %copy-start.9 = (bf16[2,2048]{1,0:T(2,128)(2,1)S(1)}, bf16[2,2048]{1,0:T(2,128)(2,1)}, u32[]{:S(2)}) copy-start(bf16[2,2048]{1,0:T(2,128)(2,1)} %param.5) | copy-start | bytes 24580
  70.2 55.5 %copy-start.10 = (f32[2048]{0:T(1024)S(1)}, f32[2048]{0:T(1024)}, u32[]{:S(2)}) copy-start(f32[2048]{0:T(1024)} %param.9) | copy-start | bytes 24580
  70.2 65.5 %copy-start.4 = (s32[1024]{0:T(1024)S(1)}, s32[1024]{0:T(1024)}, u32[]{:S(2)}) copy-start(s32[1024]{0:T(1024)} %copy-done.3) | copy-start | bytes 12292
  140.1 19.2 %collective-permute-start = (bf16[1,16,2,64]{3,2,1,0:T(2,128)(2,1)S(1)}, bf16[1,16,2,64]{3,2,1,0:T(2,128)(2,1)S(1)}, u32[]{:S(2)}, u32[]{:S(2)}) collective-permute-start(bf16[1,16,2,64]{3,2,1,0:T(2,128)(2,1)S(1)} %bitcast.61), channel_id=1, source_target_pairs={{0,24},{8,0},{16,8},{24,16},{1,25},{9,1},{17,9},{25,17},{2,26},{10... | collective-permute-start | bytes 12296 | tf_op jit(solution)/shard_map/ppermute | solution.py:15
  159.3 4.7 %collective-permute-start.1 = (bf16[2,16,2,64]{3,2,1,0:T(2,128)(2,1)S(1)}, bf16[2,16,2,64]{3,2,1,0:T(2,128)(2,1)S(1)}, u32[]{:S(2)}, u32[]{:S(2)}) collective-permute-start(bf16[2,16,2,64]{3,2,1,0:T(2,128)(2,1)S(1)} %pad_maximum_fusion), channel_id=1, source_target_pairs={{0,16},{8,24},{16,0},{24,8},{1,17},{9,25},{17,1},{25,9},{2,18},{10... | collective-permute-start | bytes 24584 | tf_op jit(solution)/shard_map/ppermute | solution.py:15
  164.1 9.2 %all-to-all-start = ((bf16[4,2,8192]{2,1,0:T(2,128)(2,1)}), bf16[4,2,8192]{2,1,0:T(2,128)(2,1)S(1)}, u32[]{:S(2)}, u32[]{:S(2)}) async-start(bf16[4,2,8192]{2,1,0:T(2,128)(2,1)} %reshape.171), calls=%async_computation | async-start | bytes 262144 | tf_op jit(solution)/shard_map/all_to_all | solution.py:86
Sparse Core Ops, SparseCore 0:
  72.3 53.3 all-reduce.2
